TPU v7x, 32 devices: a whole 2x2x4 slice. The times are simulated.
32 devices in a mesh: dp: 8 (over y, x, core), tensor: 4 (over z).
Axes of the slice: x: 2, y: 2, z: 4, core: 2. Of those that a mesh axis runs over, the one named last changes fastest.
Arguments:
- x_in: bfloat16 [16384, 1024], P(('dp', 'tensor')), may hold values from -6 to 6
- in_w: bfloat16 [1024, 3, 1024], P('dp', None, 'tensor'), may hold values from -0.1875 to 0.1875
- out_w: bfloat16 [1024, 1024], P('tensor', 'dp'), may hold values from -0.1875 to 0.1875
- gate_w: bfloat16 [1024, 4608], P('dp', 'tensor'), may hold values from -0.1875 to 0.1875
- up_w: bfloat16 [1024, 4608], P('dp', 'tensor'), may hold values from -0.1875 to 0.1875
- down_w: bfloat16 [4608, 1024], P('tensor', 'dp'), may hold values from -0.125 to 0.125
- conv_w: bfloat16 [3, 1024], replicated, may hold values from -3 to 3
- gain1: bfloat16 [1024], replicated, may hold values from 0.25 to 1.75
- gain2: bfloat16 [1024], replicated, may hold values from 0.25 to 1.75
- d_out: bfloat16 [16384, 1024], P(('dp', 'tensor')), may hold values from -6 to 6
Outputs:
- block_out: bfloat16 [16384, 1024], P(('dp', 'tensor'))
- d_x: bfloat16 [16384, 1024], P(('dp', 'tensor'))
- grad_in: float32 [1024, 3, 1024], P('dp', None, 'tensor')
- grad_out: float32 [1024, 1024], P('tensor', 'dp')
- grad_gate: float32 [1024, 4608], P('dp', 'tensor')
- grad_up: float32 [1024, 4608], P('dp', 'tensor')
- grad_down: float32 [4608, 1024], P('tensor', 'dp')
- grad_conv: float32 [3, 1024], replicated
- grad_gain1: float32 [1024], replicated
- grad_gain2: float32 [1024], replicated
All inputs are finite; a program needn't handle non-finite values.
Results may differ from a plain program's by a relative error of at most 0.018.
Values may be sent and summed in bfloat16 or wider, within the bound.
No kernel may reach another device: no remote copies, remote signals or barrier semaphores. Data moves between devices by JAX's collectives and lax.ppermute only.
A program may use at most 192 MiB of HBM per device.

v0:
```python
import jax
import jax.numpy as jnp
from jax import lax
from jax.sharding import PartitionSpec as P

LEN = 1024
epsilon = 1e-05


def in_blocks(x, dim, devices):
    before, after = (x.shape[:dim], x.shape[dim + 1 :])
    return jnp.moveaxis(x.reshape(*before, devices, -1, *after), dim, 0)


def sum_at_owner(x, axis, dim):
    tiles = in_blocks(x, dim, lax.axis_size(axis))
    arrived = lax.all_to_all(tiles, axis, split_axis=0, concat_axis=0, tiled=True)
    return arrived.astype(jnp.float32).sum(axis=0)


def norm_rows(values):
    scale = lax.rsqrt(jnp.mean(values * values, axis=-1, keepdims=True) + epsilon)
    return (values * scale, scale)


def norm_back(grad_h, normed, scale, gain):
    grad_n = grad_h * gain
    inner = jnp.mean(grad_n * normed, axis=-1, keepdims=True)
    return scale * (grad_n - normed * inner)


def delayed(values, steps_back):
    length = values.shape[1]
    padded = jnp.pad(values, ((0, 0), (steps_back, 0), (0, 0)))
    return padded[:, :length]


def advanced(values, steps_ahead):
    padded = jnp.pad(values, ((0, 0), (0, steps_ahead), (0, 0)))
    return padded[:, steps_ahead:]


def body(x_in, in_w, out_w, gate_w, up_w, down_w, conv_w, gain1, gain2, d_out):
    in_full, out_full, gate_full, up_full, down_full = (
        lax.all_gather(in_w, "dp", axis=0, tiled=True),
        lax.all_gather(out_w, "dp", axis=1, tiled=True),
        lax.all_gather(gate_w, "dp", axis=0, tiled=True),
        lax.all_gather(up_w, "dp", axis=0, tiled=True),
        lax.all_gather(down_w, "dp", axis=1, tiled=True),
    )
    model_width = x_in.shape[1]
    width = out_full.shape[0]
    offset = lax.axis_index("tensor") * width
    kernel = lax.dynamic_slice_in_dim(conv_w, offset, width, 1).astype(jnp.float32)
    gain_one = gain1.astype(jnp.float32)
    gain_two = gain2.astype(jnp.float32)
    tokens = x_in.astype(jnp.float32)
    normed_one, scale_one = norm_rows(tokens)
    first = (normed_one * gain_one).astype(jnp.bfloat16)
    first_all = lax.all_gather(first, "tensor", axis=0, tiled=True)
    group_rows = first_all.shape[0]
    seq_count = group_rows // LEN
    projected = jnp.einsum("td,dkc->tkc", first_all, in_full, preferred_element_type=jnp.float32)
    b_part = projected[:, 0].reshape(seq_count, LEN, width)
    c_part = projected[:, 1].reshape(seq_count, LEN, width)
    x_part = projected[:, 2].reshape(seq_count, LEN, width)
    mixed_in = b_part * x_part
    back_one = delayed(mixed_in, 1)
    back_two = delayed(mixed_in, 2)
    conv_out = kernel[2] * mixed_in + kernel[1] * back_one + kernel[0] * back_two
    branch = (c_part * conv_out).reshape(group_rows, width).astype(jnp.bfloat16)
    rows_now = branch
    mixed = lax.psum_scatter(
        jnp.dot(rows_now, out_full, preferred_element_type=jnp.float32).astype(jnp.bfloat16),
        "tensor",
        scatter_dimension=0,
        tiled=True,
    ).astype(jnp.float32)
    resid = tokens + mixed
    normed_two, scale_two = norm_rows(resid)
    second = (normed_two * gain_two).astype(jnp.bfloat16)
    second_all = lax.all_gather(second, "tensor", axis=0, tiled=True)
    gate = jnp.dot(second_all, gate_full, preferred_element_type=jnp.float32)
    up_val = jnp.dot(second_all, up_full, preferred_element_type=jnp.float32)
    sigma = jax.nn.sigmoid(gate)
    silu_gate = gate * sigma
    hidden = (silu_gate * up_val).astype(jnp.bfloat16)
    rows_now = hidden
    ffn = lax.psum_scatter(
        jnp.dot(rows_now, down_full, preferred_element_type=jnp.float32).astype(jnp.bfloat16),
        "tensor",
        scatter_dimension=0,
        tiled=True,
    ).astype(jnp.float32)
    block_out = (resid + ffn).astype(jnp.bfloat16)
    cot_all = lax.all_gather(d_out, "tensor", axis=0, tiled=True)
    d_hidden = jnp.einsum("td,fd->tf", cot_all, down_full, preferred_element_type=jnp.float32)
    d_gate = (d_hidden * up_val * sigma * (1.0 + gate * (1.0 - sigma))).astype(jnp.bfloat16)
    d_up = (d_hidden * silu_gate).astype(jnp.bfloat16)
    grad_down = jnp.einsum("tf,td->fd", hidden, cot_all, preferred_element_type=jnp.float32)
    grad_gate = jnp.einsum("td,tf->df", second_all, d_gate, preferred_element_type=jnp.float32)
    grad_up = jnp.einsum("td,tf->df", second_all, d_up, preferred_element_type=jnp.float32)
    grad_gate, grad_up, grad_down = (
        lax.psum_scatter(grad_gate, "dp", scatter_dimension=0, tiled=True),
        lax.psum_scatter(grad_up, "dp", scatter_dimension=0, tiled=True),
        lax.psum_scatter(grad_down, "dp", scatter_dimension=1, tiled=True),
    )
    part_gate = jnp.einsum("tf,df->td", d_gate, gate_full, preferred_element_type=jnp.float32)
    part_up = jnp.einsum("tf,df->td", d_up, up_full, preferred_element_type=jnp.float32)
    d_second = lax.psum_scatter(
        (part_gate + part_up).astype(jnp.bfloat16), "tensor", scatter_dimension=0, tiled=True
    ).astype(jnp.float32)
    gain_two_part = jnp.sum(d_second * normed_two, axis=0)
    d_resid = d_out.astype(jnp.float32) + norm_back(d_second, normed_two, scale_two, gain_two)
    d_mixed = lax.all_gather(d_resid.astype(jnp.bfloat16), "tensor", axis=0, tiled=True)
    grad_out = jnp.einsum("tc,td->cd", branch, d_mixed, preferred_element_type=jnp.float32)
    d_branch = jnp.einsum(
        "td,cd->tc", d_mixed, out_full, preferred_element_type=jnp.float32
    ).reshape(seq_count, LEN, width)
    d_conv = d_branch * c_part
    d_c = d_branch * conv_out
    d_mixin = kernel[2] * d_conv + kernel[1] * advanced(d_conv, 1) + kernel[0] * advanced(d_conv, 2)
    tap_two = jnp.sum(d_conv * mixed_in, axis=(0, 1))
    tap_one = jnp.sum(d_conv * back_one, axis=(0, 1))
    tap_zero = jnp.sum(d_conv * back_two, axis=(0, 1))
    d_b = d_mixin * x_part
    d_xpart = d_mixin * b_part
    d_proj = (
        jnp.stack([d_b, d_c, d_xpart], axis=2).reshape(group_rows, 3, width).astype(jnp.bfloat16)
    )
    grad_in = jnp.einsum("td,tkc->dkc", first_all, d_proj, preferred_element_type=jnp.float32)
    grad_in, grad_out = (
        sum_at_owner(grad_in.astype(jnp.bfloat16), "dp", 0),
        sum_at_owner(grad_out.astype(jnp.bfloat16), "dp", 1),
    )
    rows_now = d_proj
    d_first = lax.psum_scatter(
        jnp.einsum("tkc,dkc->td", rows_now, in_full, preferred_element_type=jnp.float32).astype(
            jnp.bfloat16
        ),
        "tensor",
        scatter_dimension=0,
        tiled=True,
    ).astype(jnp.float32)
    gain_one_part = jnp.sum(d_first * normed_one, axis=0)
    d_x = (d_resid + norm_back(d_first, normed_one, scale_one, gain_one)).astype(jnp.bfloat16)
    taps_local = jnp.stack([tap_zero, tap_one, tap_two], axis=0)
    taps_whole = lax.dynamic_update_slice_in_dim(
        jnp.zeros((3, model_width), jnp.float32), taps_local, offset, 1
    )
    grad_gain1, grad_gain2, grad_conv = lax.psum(
        (gain_one_part, gain_two_part, taps_whole), ("dp", "tensor")
    )
    return (
        block_out,
        d_x,
        grad_in,
        grad_out,
        grad_gate,
        grad_up,
        grad_down,
        grad_conv,
        grad_gain1,
        grad_gain2,
    )


def solution(mesh):
    in_specs = (
        P(("dp", "tensor"), None),
        P("dp", None, "tensor"),
        P("tensor", "dp"),
        P("dp", "tensor"),
        P("dp", "tensor"),
        P("tensor", "dp"),
        P(),
        P(),
        P(),
        P(("dp", "tensor"), None),
    )
    out_specs = (
        P(("dp", "tensor"), None),
        P(("dp", "tensor"), None),
        P("dp", None, "tensor"),
        P("tensor", "dp"),
        P("dp", "tensor"),
        P("dp", "tensor"),
        P("tensor", "dp"),
        P(),
        P(),
        P(),
    )
    return jax.shard_map(body, mesh=mesh, in_specs=in_specs, out_specs=out_specs, check_vma=False)
```

profile of v0, /device:TPU:0, one launch (start us, length us, event | category | flops | bytes accessed | tf_op | source)
XLA Modules:
  0.0 1019.6 jit_solution(11951078540977682232)
XLA Ops:
  7.2 0.7 all-gather.11.cloned.1.call-update
  8.0 0.7 convert_element_type.91
  8.6 1.5 fusion.26
  10.2 2.5 fusion.23
  12.8 0.7 dynamic-slice_convert_fusion
  13.5 12.6 %all_gather.29 = bf16[256,1024]{1,0:T(8,128)(2,1)S(1)} all-gather(bf16[256,128]{1,0:T(8,128)(2,1)S(1)} %copy-done.21), channel_id=1, replica_groups=mesh['dp'=8,'tensor'=4] {'dp'}, dimensions={1}, use_global_device_ids=true | all-gather | bytes 589824 | tf_op jit(solution)/shard_map/all_gather | solution.py:46
  26.1 12.9 %all-gather.11.cloned.1.call-done = bf16[1024,3,256]{2,0,1:T(8,128)(2,1)} async-done(((bf16[128,3,256]{2,0,1:T(8,128)(2,1)}), bf16[1024,3,256]{2,0,1:T(8,128)(2,1)}) %all-gather.11.cloned.1.call-update) | async-done | bytes 1572880 | tf_op jit(solution)/shard_map/all_gather | solution.py:45
  39.0 82.9 %all-gather.9.cloned.1.call-done = bf16[2048,1024]{1,0:T(8,128)(2,1)} async-done(((bf16[512,1024]{1,0:T(8,128)(2,1)}), bf16[2048,1024]{1,0:T(8,128)(2,1)}) %all-gather.9.cloned.1.call-update) | async-done | bytes 4194320 | tf_op jit(solution)/shard_map/all_gather | solution.py:60
  122.0 5.6 fusion.3
  128.1 2.2 copy-done.14
  130.6 1.0 copy-done.2
  131.6 0.7 copy-done.6
  132.3 0.6 copy-done.8
  132.9 2.1 multiply_convert_fusion.7
  135.0 1.0 copy-done.13
  136.0 3.3 convolution_convert_fusion.1
  140.1 74.8 %reduce-scatter.8.cloned.1.call-done = bf16[512,1024]{1,0:T(8,128)(2,1)} async-done(((bf16[2048,1024]{1,0:T(8,128)(2,1)}), bf16[512,1024]{1,0:T(8,128)(2,1)}) %reduce-scatter.8.cloned.1.call-update) | async-done | bytes 1048592 | tf_op jit(solution)/shard_map/reduce_scatter | solution.py:73
  214.8 1.7 multiply_reduce_fusion.2
  216.6 1.4 multiply_convert_fusion.6
  218.6 0.7 all-gather.19.cloned.1.call-update
  219.3 0.7 all-gather.21.cloned.1.call-update
  220.1 0.6 reduce-scatter.12.cloned.1.call-start
  220.6 25.7 %all-gather.15.cloned.1.call-done = bf16[1024,1152]{1,0:T(8,128)(2,1)} async-done(((bf16[128,1152]{1,0:T(8,128)(2,1)}), bf16[1024,1152]{1,0:T(8,128)(2,1)}) %all-gather.15.cloned.1.call-update) | async-done | bytes 2359312 | tf_op jit(solution)/shard_map/all_gather | solution.py:47
  246.3 82.9 %all-gather.13.cloned.1.call-done = bf16[2048,1024]{1,0:T(8,128)(2,1)} async-done(((bf16[512,1024]{1,0:T(8,128)(2,1)}), bf16[2048,1024]{1,0:T(8,128)(2,1)}) %all-gather.13.cloned.1.call-update) | async-done | bytes 4194320 | tf_op jit(solution)/shard_map/all_gather | solution.py:82
  329.2 10.3 %fusion.39 = f32[2048,1152]{1,0:T(8,128)} fusion(bf16[2048,1024]{1,0:T(8,128)(2,1)} %all-gather.13.cloned.1.call-done, bf16[1024,1152]{1,0:T(8,128)(2,1)} %all-gather.15.cloned.1.call-done), kind=kOutput, calls=%fused_computation.77 | convolution fusion | flops 4831838208 | bytes 15990784 | tf_op jit(solution)/shard_map/dot_general | solution.py:83
  339.4 19.2 %all-gather.17.cloned.1.call-done = bf16[1024,1152]{1,0:T(8,128)(2,1)} async-done(((bf16[128,1152]{1,0:T(8,128)(2,1)}), bf16[1024,1152]{1,0:T(8,128)(2,1)}) %all-gather.17.cloned.1.call-update) | async-done | bytes 2359312 | tf_op jit(solution)/shard_map/all_gather | solution.py:48
  358.6 10.3 %fusion.40 = f32[2048,1152]{1,0:T(8,128)} fusion(bf16[2048,1024]{1,0:T(8,128)(2,1)} %all-gather.13.cloned.1.call-done, bf16[1024,1152]{1,0:T(8,128)(2,1)} %all-gather.17.cloned.1.call-done), kind=kOutput, calls=%fused_computation.78 | convolution fusion | flops 4831838208 | bytes 15990784 | tf_op jit(solution)/shard_map/dot_general | solution.py:84
  368.9 21.1 %all-gather.19.cloned.1.call-done = bf16[1152,1024]{1,0:T(8,128)(2,1)} async-done(((bf16[1152,128]{1,0:T(8,128)(2,1)}), bf16[1152,1024]{1,0:T(8,128)(2,1)}) %all-gather.19.cloned.1.call-update) | async-done | bytes 2359312 | tf_op jit(solution)/shard_map/all_gather | solution.py:49
  390.1 82.4 %all-gather.21.cloned.1.call-done = bf16[2048,1024]{1,0:T(8,128)(2,1)} async-done(((bf16[512,1024]{1,0:T(8,128)(2,1)}), bf16[2048,1024]{1,0:T(8,128)(2,1)}) %all-gather.21.cloned.1.call-update) | async-done | bytes 4194320 | tf_op jit(solution)/shard_map/all_gather | solution.py:96
  472.5 17.8 %multiply_convert_fusion = (bf16[2048,1152]{1,0:T(8,128)(2,1)}, bf16[2048,1152]{1,0:T(8,128)(2,1)}, bf16[2048,1152]{1,0:T(8,128)(2,1)}) fusion(f32[2048,1152]{1,0:T(8,128)} %fusion.39, f32[2048,1152]{1,0:T(8,128)} %fusion.40, bf16[2048,1024]{1,0:T(8,128)(2,1)} %all-gather.21.cloned.1.call-done, bf16[1152,1024]{1,0:T(8,128)(2,1)} %all-gather.19.cloned.1.call-done), kind=kOutput, calls=%fused_computation | convolution fusion | flops 4867227648 | bytes 39583744 | tf_op jit(solution)/shard_map/td,fd->tf/dot_general | solution.py:97
  490.4 7.7 fusion.41
  498.0 7.7 add_convert_fusion
  505.9 75.4 %reduce-scatter.12.cloned.1.call-done = bf16[512,1024]{1,0:T(8,128)(2,1)} async-done(((bf16[2048,1024]{1,0:T(8,128)(2,1)}), bf16[512,1024]{1,0:T(8,128)(2,1)}) %reduce-scatter.12.cloned.1.call-update) | async-done | bytes 1048592 | tf_op jit(solution)/shard_map/reduce_scatter | solution.py:110
  581.3 2.2 fusion.22
  583.5 1.8 fusion.35
  585.4 81.4 %all-gather.23.cloned.1.call-done = bf16[2048,1024]{1,0:T(8,128)(2,1)} async-done(((bf16[512,1024]{1,0:T(8,128)(2,1)}), bf16[2048,1024]{1,0:T(8,128)(2,1)}) %all-gather.23.cloned.1.call-update) | async-done | bytes 4194320 | tf_op jit(solution)/shard_map/all_gather | solution.py:115
  666.7 5.8 fusion.27
  672.8 0.8 multiply_reduce_fusion.1
  673.6 0.8 copy-done.3
  674.4 0.8 multiply_convert_fusion.5
  675.1 0.8 copy-done.7
  676.4 0.9 copy-done.17
  677.5 5.0 bitcast_convert_fusion
  682.5 9.5 convolution_convert_fusion
  692.1 10.5 %fusion.42 = f32[1024,1152]{1,0:T(8,128)} fusion(bf16[2048,1024]{1,0:T(8,128)(2,1)} %all-gather.13.cloned.1.call-done, bf16[2048,1152]{1,0:T(8,128)(2,1)} %get-tuple-element.25), kind=kOutput, calls=%fused_computation.80 | convolution fusion | flops 4831838208 | bytes 13631488 | tf_op jit(solution)/shard_map/td,tf->df/dot_general | solution.py:101
  702.6 10.3 %fusion.43 = f32[1024,1152]{1,0:T(8,128)} fusion(bf16[2048,1024]{1,0:T(8,128)(2,1)} %all-gather.13.cloned.1.call-done, bf16[2048,1152]{1,0:T(8,128)(2,1)} %get-tuple-element.24), kind=kOutput, calls=%fused_computation.81 | convolution fusion | flops 4831838208 | bytes 13631488 | tf_op jit(solution)/shard_map/td,tf->df/dot_general | solution.py:102
  713.0 9.8 fusion.44
  722.8 3.8 fusion.32
  726.6 0.9 copy.28
  727.5 4.4 all-to-all-start.1
  731.9 6.7 fusion.29
  738.6 1.3 copy.22
  739.9 1.8 all-to-all-done.1
  741.7 4.3 all-to-all-start
  746.1 1.8 convert_reduce_fusion.1
  747.9 19.2 %all-to-all-done = bf16[8,128,3,256]{3,1,2,0:T(8,128)(2,1)} async-done(((bf16[8,128,3,256]{3,1,2,0:T(8,128)(2,1)}), bf16[8,128,3,256]{3,1,2,0:T(8,128)(2,1)}, u32[]{:S(2)}, u32[]{:S(2)}) %all-to-all-start) | async-done | bytes 1572896 | tf_op jit(solution)/shard_map/all_to_all | solution.py:17
  767.1 2.5 convert_reduce_fusion
  769.6 2.0 fusion.25
  771.6 42.7 %all-reduce.4 = (f32[3,1024]{1,0:T(4,128)}, f32[1024]{0:T(1024)}, f32[1024]{0:T(1024)}) all-reduce(f32[3,1024]{1,0:T(4,128)S(1)} %maximum_dynamic-update-slice_fusion, f32[1024]{0:T(1024)S(1)} %get-tuple-element.14, f32[1024]{0:T(1024)S(1)} %get-tuple-element.12), channel_id=1, replica_groups=mesh['dp'=8,'tensor'=4] {'dp','tensor'}, use_global_device_ids=true, to_apply=%region_16.17 | all-reduce | flops 5120 | bytes 40960 | tf_op jit(solution)/shard_map/psum | solution.py:151
  814.3 24.2 %reduce-scatter.10.cloned.1.call-done = bf16[512,1024]{1,0:T(8,128)(2,1)} async-done(((bf16[2048,1024]{1,0:T(8,128)(2,1)}), bf16[512,1024]{1,0:T(8,128)(2,1)}) %reduce-scatter.10.cloned.1.call-update) | async-done | bytes 1048592 | tf_op jit(solution)/shard_map/reduce_scatter | solution.py:89
  838.5 4.1 fusion.18
  842.7 54.2 %reduce-scatter.16.cloned.1.call-done = f32[128,1152]{1,0:T(8,128)} async-done(((f32[1024,1152]{1,0:T(8,128)}), f32[128,1152]{1,0:T(8,128)}) %reduce-scatter.16.cloned.1.call-update) | async-done | bytes 589840 | tf_op jit(solution)/shard_map/reduce_scatter | solution.py:104
  896.9 58.2 %reduce-scatter.18.cloned.1.call-done = f32[128,1152]{1,0:T(8,128)} async-done(((f32[1024,1152]{1,0:T(8,128)}), f32[128,1152]{1,0:T(8,128)}) %reduce-scatter.18.cloned.1.call-update) | async-done | bytes 589840 | tf_op jit(solution)/shard_map/reduce_scatter | solution.py:105
  955.1 57.8 %reduce-scatter.20.cloned.1.call-done = f32[1152,128]{1,0:T(8,128)} async-done(((f32[1152,1024]{1,0:T(8,128)}), f32[1152,128]{1,0:T(8,128)}) %reduce-scatter.20.cloned.1.call-update) | async-done | bytes 589840 | tf_op jit(solution)/shard_map/reduce_scatter | solution.py:106
  (88 shorter events, 3.4 us)
Async XLA Ops:
  7.2 31.9 %all-gather.11.cloned.1.call-start = ((), (), s32[]{:S(2)}) async-start(), calls=%async_computation.10 | async-start | bytes 1769472 | tf_op jit(solution)/shard_map/all_gather | solution.py:45
  7.9 114.1 %all-gather.9.cloned.1.call-start = ((), (), s32[]{:S(2)}) async-start(), calls=%async_computation.9 | async-start | bytes 5242880 | tf_op jit(solution)/shard_map/all_gather | solution.py:60
  8.6 4.8 copy-start.19
  8.6 4.8 copy-start.21
  10.2 111.8 %copy-start.22 = (f32[512]{0:T(512)}, f32[512]{0:T(512)S(1)}, u32[]{:S(2)}) copy-start(f32[512]{0:T(512)S(1)} %add_rsqrt_fusion.1) | copy-start | bytes 6148
  12.7 202.1 %reduce-scatter.8.cloned.1.call-start = ((), (), s32[]{:S(2)}) async-start(), calls=%async_computation.11 | async-start | bytes 5242880 | tf_op jit(solution)/shard_map/reduce_scatter | solution.py:73
  26.1 108.9 %copy-start.15 = (bf16[256,1024]{1,0:T(8,128)(2,1)}, bf16[256,1024]{1,0:T(8,128)(2,1)S(1)}, u32[]{:S(2)}) copy-start(bf16[256,1024]{1,0:T(8,128)(2,1)S(1)} %all_gather.29) | copy-start | bytes 1572868
  127.6 2.7 copy-start.14
  130.3 1.3 copy-start.2
  130.3 2.0 copy-start.6
  130.3 2.6 copy-start.8
  132.3 2.8 copy-start.4
  135.0 1.0 copy-start.13
  139.4 0.7 copy-start.24
  139.4 75.5 %copy-start = (bf16[512,1024]{1,0:T(8,128)(2,1)S(1)}, bf16[512,1024]{1,0:T(8,128)(2,1)}, u32[]{:S(2)}) copy-start(bf16[512,1024]{1,0:T(8,128)(2,1)} %param.10) | copy-start | bytes 3145732
  139.4 106.9 %all-gather.15.cloned.1.call-start = ((), (), s32[]{:S(2)}) async-start(), calls=%async_computation.13 | async-start | bytes 2654208 | tf_op jit(solution)/shard_map/all_gather | solution.py:47
  140.0 189.2 %all-gather.13.cloned.1.call-start = ((), (), s32[]{:S(2)}) async-start(), calls=%async_computation.12 | async-start | bytes 5242880 | tf_op jit(solution)/shard_map/all_gather | solution.py:82
  214.8 1.7 copy-start.1
  218.0 140.7 %all-gather.17.cloned.1.call-start = ((), (), s32[]{:S(2)}) async-start(), calls=%async_computation.14 | async-start | bytes 2654208 | tf_op jit(solution)/shard_map/all_gather | solution.py:48
  218.6 171.5 %all-gather.19.cloned.1.call-start = ((), (), s32[]{:S(2)}) async-start(), calls=%async_computation.15 | async-start | bytes 2654208 | tf_op jit(solution)/shard_map/all_gather | solution.py:49
  219.3 253.2 %all-gather.21.cloned.1.call-start = ((), (), s32[]{:S(2)}) async-start(), calls=%async_computation.17 | async-start | bytes 5242880 | tf_op jit(solution)/shard_map/all_gather | solution.py:96
  220.1 361.2 %reduce-scatter.12.cloned.1.call-start = ((), (), s32[]{:S(2)}) async-start(), calls=%async_computation.18 | async-start | bytes 5242880 | tf_op jit(solution)/shard_map/reduce_scatter | solution.py:110
  472.5 17.8 %copy-start.25 = (bf16[1024,1152]{1,0:T(8,128)(2,1)S(1)}, bf16[1024,1152]{1,0:T(8,128)(2,1)}, u32[]{:S(2)}) copy-start(bf16[1024,1152]{1,0:T(8,128)(2,1)} %all-gather.15.cloned.1.call-done) | copy-start | bytes 7077892
  490.3 7.7 copy-start.26
  490.3 7.7 copy-start.28
  505.8 77.7 %copy-start.10 = (bf16[512,1024]{1,0:T(8,128)(2,1)S(1)}, bf16[512,1024]{1,0:T(8,128)(2,1)}, u32[]{:S(2)}) copy-start(bf16[512,1024]{1,0:T(8,128)(2,1)} %param.19) | copy-start | bytes 3145732
  505.8 160.9 %all-gather.23.cloned.1.call-start = ((), (), s32[]{:S(2)}) async-start(), calls=%async_computation.19 | async-start | bytes 5242880 | tf_op jit(solution)/shard_map/all_gather | solution.py:115
  581.3 2.2 copy-start.11
  585.3 184.2 %reduce-scatter.14.cloned.1.call-start = ((), (), s32[]{:S(2)}) async-start(), calls=%async_computation.20 | async-start | bytes 5242880 | tf_op jit(solution)/shard_map/reduce_scatter | solution.py:137
  666.7 5.8 copy-start.5
  666.7 5.8 copy-start.9
  666.7 6.0 copy-start.12
  672.8 1.6 copy-start.3
  673.6 2.8 copy-start.16
  674.4 1.6 copy-start.7
  675.1 1.3 copy-start.18
  676.0 1.5 copy-start.27
  676.4 1.0 copy-start.17
  682.5 156.0 %reduce-scatter.10.cloned.1.call-start = ((), (), s32[]{:S(2)}) async-start(), calls=%async_computation.16 | async-start | bytes 5242880 | tf_op jit(solution)/shard_map/reduce_scatter | solution.py:89
  692.0 204.9 %reduce-scatter.16.cloned.1.call-start = ((), (), s32[]{:S(2)}) async-start(), calls=%async_computation.21 | async-start | bytes 5308416 | tf_op jit(solution)/shard_map/reduce_scatter | solution.py:104
  702.6 252.5 %reduce-scatter.18.cloned.1.call-start = ((), (), s32[]{:S(2)}) async-start(), calls=%async_computation.22 | async-start | bytes 5308416 | tf_op jit(solution)/shard_map/reduce_scatter | solution.py:105
  713.0 299.9 %reduce-scatter.20.cloned.1.call-start = ((), (), s32[]{:S(2)}) async-start(), calls=%async_computation.23 | async-start | bytes 5308416 | tf_op jit(solution)/shard_map/reduce_scatter | solution.py:106
  727.5 14.2 %all-to-all-start.1 = ((bf16[8,256,128]{2,1,0:T(8,128)(2,1)}), bf16[8,256,128]{2,1,0:T(8,128)(2,1)}, u32[]{:S(2)}, u32[]{:S(2)}) async-start(bf16[8,256,128]{2,1,0:T(8,128)(2,1)} %bitcast.76), calls=%async_computation.5 | async-start | bytes 1048576 | tf_op jit(solution)/shard_map/all_to_all | solution.py:17
  741.7 25.4 %all-to-all-start = ((bf16[8,128,3,256]{3,1,2,0:T(8,128)(2,1)}), bf16[8,128,3,256]{3,1,2,0:T(8,128)(2,1)}, u32[]{:S(2)}, u32[]{:S(2)}) async-start(bf16[8,128,3,256]{3,1,2,0:T(8,128)(2,1)} %copy.22), calls=%async_computation.4 | async-start | bytes 3145728 | tf_op jit(solution)/shard_map/all_to_all | solution.py:17
  746.0 23.5 %copy-start.20 = (f32[1024]{0:T(1024)S(1)}, f32[1024]{0:T(1024)}, u32[]{:S(2)}) copy-start(f32[1024]{0:T(1024)} %copy-done.19) | copy-start | bytes 12292
  746.0 23.5 %copy-start.23 = (f32[512]{0:T(512)S(1)}, f32[512]{0:T(512)}, u32[]{:S(2)}) copy-start(f32[512]{0:T(512)} %copy-done.22) | copy-start | bytes 6148
Sparse Core Ops, SparseCore 0:
  9.9 29.0 all-gather.10
  41.2 80.7 all-gather.8
  139.5 75.2 reduce-scatter.7
  216.7 29.5 all-gather.14
  248.4 80.7 all-gather.12
  331.1 27.5 all-gather.16
  360.7 29.3 all-gather.18
  391.7 80.7 all-gather.20
  505.9 75.2 reduce-scatter.11
  585.4 81.2 all-gather.22
  682.6 75.2 reduce-scatter.13
  760.2 78.3 reduce-scatter.9
  842.5 54.3 reduce-scatter.15
  901.2 53.8 reduce-scatter.17
  958.9 53.8 reduce-scatter.19
where the time goes:
time: 1030 us; the launch traced here: 1020 us
  waiting for transfers between devices  777 us (75%)
  matrix products  124 us (12%)
  blocking collectives  55.3 us (5%)
  other arithmetic  27.4 us (3%)
  between operations  14.5 us (1%)
  local copies, waits for them, and re-layouts  11.2 us (1%)
    all_gather x1, waiting for transfers between devices, body(): first_all = lax.all_gather(first, 'tensor', axis=0, tiled=True)  82.9 us
    all_gather x1, waiting for transfers between devices, body(): second_all = lax.all_gather(second, 'tensor', axis=0, tiled=True)  82.9 us
    all_gather x1, waiting for transfers between devices, body(): cot_all = lax.all_gather(d_out, 'tensor', axis=0, tiled=True)  82.4 us
    all_gather x1, waiting for transfers between devices, body(): lax.all_gather(d_resid.astype(jnp.bfloat16), 'tensor', axis=0, tiled=True)  81.4 us
    reduce_scatter x1, waiting for transfers between devices, body(): lax.psum_scatter((part_gate + part_up).astype(jnp.bfloat16), 'tensor', sc...  75.4 us
    reduce_scatter x1, waiting for transfers between devices, body(): lax.psum_scatter(jnp.dot(rows_now, out_full, preferred_element_type=jnp.f...  74.8 us
    reduce_scatter x1, waiting for transfers between devices, body(): lax.psum_scatter(grad_up, 'dp', scatter_dimension=0, tiled=True)  58.2 us
    reduce_scatter x1, waiting for transfers between devices, body(): lax.psum_scatter(grad_down, 'dp', scatter_dimension=1, tiled=True)  57.8 us
  transfers between devices with their start and end apart: 17, of which 16 were waited for; matrix products, arithmetic and copies ran while one was open for 9% of the time, Pallas kernels for 0%

commit v1 on v0

--- a/solution.py
+++ b/solution.py
@@ -148,8 +148,14 @@
     taps_whole = lax.dynamic_update_slice_in_dim(
         jnp.zeros((3, model_width), jnp.float32), taps_local, offset, 1
     )
-    grad_gain1, grad_gain2, grad_conv = lax.psum(
-        (gain_one_part, gain_two_part, taps_whole), ("dp", "tensor")
+
+    def draft_record_for(packet, group_axis, device_axis):
+        for num in (group_axis, device_axis):
+            packet = lax.psum(packet, axis_name=num)
+        return packet
+
+    grad_gain1, grad_gain2, grad_conv = draft_record_for(
+        (gain_one_part, gain_two_part, taps_whole), "tensor", "dp"
     )
     return (
         block_out,

time: 1030 us -> 1020 us (level)
    psum x1 -> x2, blocking collectives: 42.7 us -> 41 us  [draft_record_for(): packet = lax.psum(packet, axis_name=num)]
where the time goes in v1:
time: 1020 us
  waiting for transfers between devices  778 us (76%)
  matrix products  124 us (12%)
  blocking collectives  54.6 us (5%)
  other arithmetic  27.3 us (3%)
  between operations  14.5 us (1%)
    all_gather x1, waiting for transfers between devices, body(): first_all = lax.all_gather(first, 'tensor', axis=0, tiled=True)  82.9 us
    all_gather x1, waiting for transfers between devices, body(): second_all = lax.all_gather(second, 'tensor', axis=0, tiled=True)  82.9 us
    all_gather x1, waiting for transfers between devices, body(): cot_all = lax.all_gather(d_out, 'tensor', axis=0, tiled=True)  82.4 us
    all_gather x1, waiting for transfers between devices, body(): lax.all_gather(d_resid.astype(jnp.bfloat16), 'tensor', axis=0, tiled=True)  81.4 us
    reduce_scatter x1, waiting for transfers between devices, body(): lax.psum_scatter((part_gate + part_up).astype(jnp.bfloat16), 'tensor', sc...  75.4 us
    reduce_scatter x1, waiting for transfers between devices, body(): lax.psum_scatter(jnp.dot(rows_now, out_full, preferred_element_type=jnp.f...  74.8 us
    reduce_scatter x1, waiting for transfers between devices, body(): lax.psum_scatter(grad_up, 'dp', scatter_dimension=0, tiled=True)  58.2 us
    reduce_scatter x1, waiting for transfers between devices, body(): lax.psum_scatter(grad_down, 'dp', scatter_dimension=1, tiled=True)  57.8 us
  transfers between devices with their start and end apart: 17, of which 16 were waited for; matrix products, arithmetic and copies ran while one was open for 9% of the time, Pallas kernels for 0%

profile of v1, /device:TPU:0, one launch (start us, length us, event | category | flops | bytes accessed | tf_op | source)
XLA Modules:
  0.0 1019.0 jit_solution(11468530918710723090)
XLA Ops:
  7.2 0.7 all-gather.11.cloned.1.call-update
  8.0 0.7 convert_element_type.91
  8.6 1.5 fusion.26
  10.2 2.5 fusion.23
  12.8 0.7 dynamic-slice_convert_fusion
  13.5 13.6 %all_gather.29 = bf16[256,1024]{1,0:T(8,128)(2,1)} all-gather(bf16[256,128]{1,0:T(8,128)(2,1)S(1)} %copy-done.21), channel_id=1, replica_groups=mesh['dp'=8,'tensor'=4] {'dp'}, dimensions={1}, use_global_device_ids=true | all-gather | bytes 589824 | tf_op jit(solution)/shard_map/all_gather | solution.py:46
  27.1 12.3 %all-gather.11.cloned.1.call-done = bf16[1024,3,256]{2,0,1:T(8,128)(2,1)} async-done(((bf16[128,3,256]{2,0,1:T(8,128)(2,1)}), bf16[1024,3,256]{2,0,1:T(8,128)(2,1)}) %all-gather.11.cloned.1.call-update) | async-done | bytes 1572880 | tf_op jit(solution)/shard_map/all_gather | solution.py:45
  39.4 82.9 %all-gather.9.cloned.1.call-done = bf16[2048,1024]{1,0:T(8,128)(2,1)} async-done(((bf16[512,1024]{1,0:T(8,128)(2,1)}), bf16[2048,1024]{1,0:T(8,128)(2,1)}) %all-gather.9.cloned.1.call-update) | async-done | bytes 4194320 | tf_op jit(solution)/shard_map/all_gather | solution.py:60
  122.3 5.6 fusion.3
  128.4 2.2 copy-done.14
  130.9 1.0 copy-done.2
  131.9 0.7 copy-done.6
  132.6 0.6 copy-done.8
  133.2 2.1 multiply_convert_fusion.7
  135.3 3.3 convolution_convert_fusion.1
  139.4 74.8 %reduce-scatter.8.cloned.1.call-done = bf16[512,1024]{1,0:T(8,128)(2,1)} async-done(((bf16[2048,1024]{1,0:T(8,128)(2,1)}), bf16[512,1024]{1,0:T(8,128)(2,1)}) %reduce-scatter.8.cloned.1.call-update) | async-done | bytes 1048592 | tf_op jit(solution)/shard_map/reduce_scatter | solution.py:73
  214.2 1.7 multiply_reduce_fusion.2
  215.9 1.4 multiply_convert_fusion.6
  217.9 0.7 all-gather.19.cloned.1.call-update
  218.7 0.7 all-gather.21.cloned.1.call-update
  219.4 0.6 reduce-scatter.12.cloned.1.call-start
  219.9 25.7 %all-gather.15.cloned.1.call-done = bf16[1024,1152]{1,0:T(8,128)(2,1)} async-done(((bf16[128,1152]{1,0:T(8,128)(2,1)}), bf16[1024,1152]{1,0:T(8,128)(2,1)}) %all-gather.15.cloned.1.call-update) | async-done | bytes 2359312 | tf_op jit(solution)/shard_map/all_gather | solution.py:47
  245.6 82.9 %all-gather.13.cloned.1.call-done = bf16[2048,1024]{1,0:T(8,128)(2,1)} async-done(((bf16[512,1024]{1,0:T(8,128)(2,1)}), bf16[2048,1024]{1,0:T(8,128)(2,1)}) %all-gather.13.cloned.1.call-update) | async-done | bytes 4194320 | tf_op jit(solution)/shard_map/all_gather | solution.py:82
  328.5 10.3 %fusion.39 = f32[2048,1152]{1,0:T(8,128)} fusion(bf16[2048,1024]{1,0:T(8,128)(2,1)} %all-gather.13.cloned.1.call-done, bf16[1024,1152]{1,0:T(8,128)(2,1)} %all-gather.15.cloned.1.call-done), kind=kOutput, calls=%fused_computation.77 | convolution fusion | flops 4831838208 | bytes 15990784 | tf_op jit(solution)/shard_map/dot_general | solution.py:83
  338.8 19.2 %all-gather.17.cloned.1.call-done = bf16[1024,1152]{1,0:T(8,128)(2,1)} async-done(((bf16[128,1152]{1,0:T(8,128)(2,1)}), bf16[1024,1152]{1,0:T(8,128)(2,1)}) %all-gather.17.cloned.1.call-update) | async-done | bytes 2359312 | tf_op jit(solution)/shard_map/all_gather | solution.py:48
  358.0 10.3 %fusion.40 = f32[2048,1152]{1,0:T(8,128)} fusion(bf16[2048,1024]{1,0:T(8,128)(2,1)} %all-gather.13.cloned.1.call-done, bf16[1024,1152]{1,0:T(8,128)(2,1)} %all-gather.17.cloned.1.call-done), kind=kOutput, calls=%fused_computation.78 | convolution fusion | flops 4831838208 | bytes 15990784 | tf_op jit(solution)/shard_map/dot_general | solution.py:84
  368.2 21.1 %all-gather.19.cloned.1.call-done = bf16[1152,1024]{1,0:T(8,128)(2,1)} async-done(((bf16[1152,128]{1,0:T(8,128)(2,1)}), bf16[1152,1024]{1,0:T(8,128)(2,1)}) %all-gather.19.cloned.1.call-update) | async-done | bytes 2359312 | tf_op jit(solution)/shard_map/all_gather | solution.py:49
  389.4 82.4 %all-gather.21.cloned.1.call-done = bf16[2048,1024]{1,0:T(8,128)(2,1)} async-done(((bf16[512,1024]{1,0:T(8,128)(2,1)}), bf16[2048,1024]{1,0:T(8,128)(2,1)}) %all-gather.21.cloned.1.call-update) | async-done | bytes 4194320 | tf_op jit(solution)/shard_map/all_gather | solution.py:96
  471.8 17.8 %multiply_convert_fusion = (bf16[2048,1152]{1,0:T(8,128)(2,1)}, bf16[2048,1152]{1,0:T(8,128)(2,1)}, bf16[2048,1152]{1,0:T(8,128)(2,1)}) fusion(f32[2048,1152]{1,0:T(8,128)} %fusion.39, f32[2048,1152]{1,0:T(8,128)} %fusion.40, bf16[2048,1024]{1,0:T(8,128)(2,1)} %all-gather.21.cloned.1.call-done, bf16[1152,1024]{1,0:T(8,128)(2,1)} %all-gather.19.cloned.1.call-done), kind=kOutput, calls=%fused_computation | convolution fusion | flops 4867227648 | bytes 39583744 | tf_op jit(solution)/shard_map/td,fd->tf/dot_general | solution.py:97
  489.7 7.7 fusion.41
  497.4 7.7 add_convert_fusion
  505.2 75.4 %reduce-scatter.12.cloned.1.call-done = bf16[512,1024]{1,0:T(8,128)(2,1)} async-done(((bf16[2048,1024]{1,0:T(8,128)(2,1)}), bf16[512,1024]{1,0:T(8,128)(2,1)}) %reduce-scatter.12.cloned.1.call-update) | async-done | bytes 1048592 | tf_op jit(solution)/shard_map/reduce_scatter | solution.py:110
  580.6 2.2 fusion.22
  582.8 1.8 fusion.35
  584.7 81.4 %all-gather.23.cloned.1.call-done = bf16[2048,1024]{1,0:T(8,128)(2,1)} async-done(((bf16[512,1024]{1,0:T(8,128)(2,1)}), bf16[2048,1024]{1,0:T(8,128)(2,1)}) %all-gather.23.cloned.1.call-update) | async-done | bytes 4194320 | tf_op jit(solution)/shard_map/all_gather | solution.py:115
  666.1 5.8 fusion.27
  672.1 0.8 multiply_reduce_fusion.1
  672.9 0.8 copy-done.3
  673.7 0.8 multiply_convert_fusion.5
  674.4 0.8 copy-done.7
  675.7 0.9 copy-done.17
  676.8 5.0 bitcast_convert_fusion
  681.8 9.5 convolution_convert_fusion
  691.4 10.5 %fusion.42 = f32[1024,1152]{1,0:T(8,128)} fusion(bf16[2048,1024]{1,0:T(8,128)(2,1)} %all-gather.13.cloned.1.call-done, bf16[2048,1152]{1,0:T(8,128)(2,1)} %get-tuple-element.28), kind=kOutput, calls=%fused_computation.80 | convolution fusion | flops 4831838208 | bytes 13631488 | tf_op jit(solution)/shard_map/td,tf->df/dot_general | solution.py:101
  702.0 10.3 %fusion.43 = f32[1024,1152]{1,0:T(8,128)} fusion(bf16[2048,1024]{1,0:T(8,128)(2,1)} %all-gather.13.cloned.1.call-done, bf16[2048,1152]{1,0:T(8,128)(2,1)} %get-tuple-element.27), kind=kOutput, calls=%fused_computation.81 | convolution fusion | flops 4831838208 | bytes 13631488 | tf_op jit(solution)/shard_map/td,tf->df/dot_general | solution.py:102
  712.4 9.7 fusion.44
  722.2 3.8 fusion.32
  726.0 0.9 copy.28
  726.9 4.4 all-to-all-start.1
  731.3 6.7 fusion.29
  738.0 1.3 copy.22
  739.3 1.7 all-to-all-done.1
  741.1 4.3 all-to-all-start
  745.4 1.8 convert_reduce_fusion.1
  747.2 19.2 %all-to-all-done = bf16[8,128,3,256]{3,1,2,0:T(8,128)(2,1)} async-done(((bf16[8,128,3,256]{3,1,2,0:T(8,128)(2,1)}), bf16[8,128,3,256]{3,1,2,0:T(8,128)(2,1)}, u32[]{:S(2)}, u32[]{:S(2)}) %all-to-all-start) | async-done | bytes 1572896 | tf_op jit(solution)/shard_map/all_to_all | solution.py:17
  766.4 2.5 convert_reduce_fusion
  768.9 2.0 fusion.25
  770.9 17.7 %all-reduce.5 = (f32[3,1024]{1,0:T(4,128)S(1)}, f32[1024]{0:T(1024)S(1)}, f32[1024]{0:T(1024)S(1)}) all-reduce(f32[3,1024]{1,0:T(4,128)S(1)} %maximum_dynamic-update-slice_fusion, f32[1024]{0:T(1024)S(1)} %get-tuple-element.14, f32[1024]{0:T(1024)S(1)} %get-tuple-element.12), channel_id=1, replica_groups=mesh['dp'=8,'tensor'=4] {'tensor'}, use_global_device_ids=true, to_apply=%region_16.17 | all-reduce | flops 5120 | bytes 40960 | tf_op jit(solution)/shard_map/psum | solution.py:154
  788.7 23.3 %all-reduce.4 = (f32[3,1024]{1,0:T(4,128)}, f32[1024]{0:T(1024)}, f32[1024]{0:T(1024)}) all-reduce(f32[3,1024]{1,0:T(4,128)S(1)} %get-tuple-element.19, f32[1024]{0:T(1024)S(1)} %get-tuple-element.20, f32[1024]{0:T(1024)S(1)} %get-tuple-element.21), channel_id=1, replica_groups=mesh['dp'=8,'tensor'=4] {'dp'}, use_global_device_ids=true, to_apply=%region_17.18 | all-reduce | flops 5120 | bytes 40960 | tf_op jit(solution)/shard_map/psum | solution.py:154
  812.0 25.8 %reduce-scatter.10.cloned.1.call-done = bf16[512,1024]{1,0:T(8,128)(2,1)} async-done(((bf16[2048,1024]{1,0:T(8,128)(2,1)}), bf16[512,1024]{1,0:T(8,128)(2,1)}) %reduce-scatter.10.cloned.1.call-update) | async-done | bytes 1048592 | tf_op jit(solution)/shard_map/reduce_scatter | solution.py:89
  837.8 4.1 fusion.18
  842.0 54.3 %reduce-scatter.16.cloned.1.call-done = f32[128,1152]{1,0:T(8,128)} async-done(((f32[1024,1152]{1,0:T(8,128)}), f32[128,1152]{1,0:T(8,128)}) %reduce-scatter.16.cloned.1.call-update) | async-done | bytes 589840 | tf_op jit(solution)/shard_map/reduce_scatter | solution.py:104
  896.2 58.2 %reduce-scatter.18.cloned.1.call-done = f32[128,1152]{1,0:T(8,128)} async-done(((f32[1024,1152]{1,0:T(8,128)}), f32[128,1152]{1,0:T(8,128)}) %reduce-scatter.18.cloned.1.call-update) | async-done | bytes 589840 | tf_op jit(solution)/shard_map/reduce_scatter | solution.py:105
  954.4 57.8 %reduce-scatter.20.cloned.1.call-done = f32[1152,128]{1,0:T(8,128)} async-done(((f32[1152,1024]{1,0:T(8,128)}), f32[1152,128]{1,0:T(8,128)}) %reduce-scatter.20.cloned.1.call-update) | async-done | bytes 589840 | tf_op jit(solution)/shard_map/reduce_scatter | solution.py:106
  (89 shorter events, 3.4 us)
Async XLA Ops:
  7.2 32.2 %all-gather.11.cloned.1.call-start = ((), (), s32[]{:S(2)}) async-start(), calls=%async_computation.10 | async-start | bytes 1769472 | tf_op jit(solution)/shard_map/all_gather | solution.py:45
  7.9 114.4 %all-gather.9.cloned.1.call-start = ((), (), s32[]{:S(2)}) async-start(), calls=%async_computation.9 | async-start | bytes 5242880 | tf_op jit(solution)/shard_map/all_gather | solution.py:60
  8.6 4.8 copy-start.19
  8.6 4.8 copy-start.21
  10.2 112.1 %copy-start.22 = (f32[512]{0:T(512)}, f32[512]{0:T(512)S(1)}, u32[]{:S(2)}) copy-start(f32[512]{0:T(512)S(1)} %add_rsqrt_fusion.1) | copy-start | bytes 6148
  12.7 201.4 %reduce-scatter.8.cloned.1.call-start = ((), (), s32[]{:S(2)}) async-start(), calls=%async_computation.11 | async-start | bytes 5242880 | tf_op jit(solution)/shard_map/reduce_scatter | solution.py:73
  128.0 2.7 copy-start.14
  130.6 1.3 copy-start.2
  130.6 2.0 copy-start.6
  130.6 2.6 copy-start.8
  132.6 2.7 copy-start.4
  133.2 2.1 copy-start.15
  135.3 3.4 copy-start.13
  138.7 0.7 copy-start.24
  138.7 75.5 %copy-start = (bf16[512,1024]{1,0:T(8,128)(2,1)S(1)}, bf16[512,1024]{1,0:T(8,128)(2,1)}, u32[]{:S(2)}) copy-start(bf16[512,1024]{1,0:T(8,128)(2,1)} %param.10) | copy-start | bytes 3145732
  138.7 106.9 %all-gather.15.cloned.1.call-start = ((), (), s32[]{:S(2)}) async-start(), calls=%async_computation.13 | async-start | bytes 2654208 | tf_op jit(solution)/shard_map/all_gather | solution.py:47
  139.3 189.2 %all-gather.13.cloned.1.call-start = ((), (), s32[]{:S(2)}) async-start(), calls=%async_computation.12 | async-start | bytes 5242880 | tf_op jit(solution)/shard_map/all_gather | solution.py:82
  214.2 1.7 copy-start.1
  217.3 140.7 %all-gather.17.cloned.1.call-start = ((), (), s32[]{:S(2)}) async-start(), calls=%async_computation.14 | async-start | bytes 2654208 | tf_op jit(solution)/shard_map/all_gather | solution.py:48
  217.9 171.5 %all-gather.19.cloned.1.call-start = ((), (), s32[]{:S(2)}) async-start(), calls=%async_computation.15 | async-start | bytes 2654208 | tf_op jit(solution)/shard_map/all_gather | solution.py:49
  218.6 253.2 %all-gather.21.cloned.1.call-start = ((), (), s32[]{:S(2)}) async-start(), calls=%async_computation.17 | async-start | bytes 5242880 | tf_op jit(solution)/shard_map/all_gather | solution.py:96
  219.4 361.2 %reduce-scatter.12.cloned.1.call-start = ((), (), s32[]{:S(2)}) async-start(), calls=%async_computation.18 | async-start | bytes 5242880 | tf_op jit(solution)/shard_map/reduce_scatter | solution.py:110
  471.8 17.8 %copy-start.25 = (bf16[1024,1152]{1,0:T(8,128)(2,1)S(1)}, bf16[1024,1152]{1,0:T(8,128)(2,1)}, u32[]{:S(2)}) copy-start(bf16[1024,1152]{1,0:T(8,128)(2,1)} %all-gather.15.cloned.1.call-done) | copy-start | bytes 7077892
  489.7 7.7 copy-start.26
  489.7 7.7 copy-start.28
  505.1 77.7 %copy-start.10 = (bf16[512,1024]{1,0:T(8,128)(2,1)S(1)}, bf16[512,1024]{1,0:T(8,128)(2,1)}, u32[]{:S(2)}) copy-start(bf16[512,1024]{1,0:T(8,128)(2,1)} %param.19) | copy-start | bytes 3145732
  505.1 160.9 %all-gather.23.cloned.1.call-start = ((), (), s32[]{:S(2)}) async-start(), calls=%async_computation.19 | async-start | bytes 5242880 | tf_op jit(solution)/shard_map/all_gather | solution.py:115
  580.6 2.2 copy-start.11
  584.6 184.3 %reduce-scatter.14.cloned.1.call-start = ((), (), s32[]{:S(2)}) async-start(), calls=%async_computation.20 | async-start | bytes 5242880 | tf_op jit(solution)/shard_map/reduce_scatter | solution.py:137
  666.1 5.8 copy-start.5
  666.1 5.8 copy-start.9
  666.1 6.0 copy-start.12
  672.1 1.6 copy-start.3
  672.9 2.8 copy-start.16
  673.7 1.6 copy-start.7
  674.4 1.3 copy-start.18
  675.3 1.5 copy-start.27
  675.7 1.0 copy-start.17
  681.8 156.0 %reduce-scatter.10.cloned.1.call-start = ((), (), s32[]{:S(2)}) async-start(), calls=%async_computation.16 | async-start | bytes 5242880 | tf_op jit(solution)/shard_map/reduce_scatter | solution.py:89
  691.3 204.9 %reduce-scatter.16.cloned.1.call-start = ((), (), s32[]{:S(2)}) async-start(), calls=%async_computation.21 | async-start | bytes 5308416 | tf_op jit(solution)/shard_map/reduce_scatter | solution.py:104
  701.9 252.5 %reduce-scatter.18.cloned.1.call-start = ((), (), s32[]{:S(2)}) async-start(), calls=%async_computation.22 | async-start | bytes 5308416 | tf_op jit(solution)/shard_map/reduce_scatter | solution.py:105
  712.4 299.9 %reduce-scatter.20.cloned.1.call-start = ((), (), s32[]{:S(2)}) async-start(), calls=%async_computation.23 | async-start | bytes 5308416 | tf_op jit(solution)/shard_map/reduce_scatter | solution.py:106
  726.9 14.2 %all-to-all-start.1 = ((bf16[8,256,128]{2,1,0:T(8,128)(2,1)}), bf16[8,256,128]{2,1,0:T(8,128)(2,1)}, u32[]{:S(2)}, u32[]{:S(2)}) async-start(bf16[8,256,128]{2,1,0:T(8,128)(2,1)} %bitcast.76), calls=%async_computation.5 | async-start | bytes 1048576 | tf_op jit(solution)/shard_map/all_to_all | solution.py:17
  741.1 25.4 %all-to-all-start = ((bf16[8,128,3,256]{3,1,2,0:T(8,128)(2,1)}), bf16[8,128,3,256]{3,1,2,0:T(8,128)(2,1)}, u32[]{:S(2)}, u32[]{:S(2)}) async-start(bf16[8,128,3,256]{3,1,2,0:T(8,128)(2,1)} %copy.22), calls=%async_computation.4 | async-start | bytes 3145728 | tf_op jit(solution)/shard_map/all_to_all | solution.py:17
  745.4 23.5 %copy-start.20 = (f32[1024]{0:T(1024)S(1)}, f32[1024]{0:T(1024)}, u32[]{:S(2)}) copy-start(f32[1024]{0:T(1024)} %copy-done.19) | copy-start | bytes 12292
  745.4 23.5 %copy-start.23 = (f32[512]{0:T(512)S(1)}, f32[512]{0:T(512)}, u32[]{:S(2)}) copy-start(f32[512]{0:T(512)} %copy-done.22) | copy-start | bytes 6148
Sparse Core Ops, SparseCore 0:
  9.9 29.4 all-gather.10
  41.5 80.7 all-gather.8
  138.8 75.2 reduce-scatter.7
  216.0 29.5 all-gather.14
  247.7 80.7 all-gather.12
  330.4 27.5 all-gather.16
  360.0 29.3 all-gather.18
  391.0 80.7 all-gather.20
  505.3 75.2 reduce-scatter.11
  584.8 81.2 all-gather.22
  681.9 75.2 reduce-scatter.13
  759.5 78.3 reduce-scatter.9
  841.9 54.3 reduce-scatter.15
  900.5 53.8 reduce-scatter.17
  958.3 53.8 reduce-scatter.19
